TPU v7x, 32 devices: a whole 2x2x4 slice. The times are simulated.
32 devices in a mesh: section: 4 (over x, core), dp: 8 (over z, y).
Axes of the slice: x: 2, y: 2, z: 4, core: 2. Of those that a mesh axis runs over, the one named last changes fastest.
Arguments:
- latent_states: bfloat16 [4, 32, 96, 2048], P('section', 'dp'), may hold values from -8 to 8
- rescale_factor: float32 [2048], replicated, may hold values from 0.25 to 1.75
- embedding_matrix: bfloat16 [2048, 128], P('section'), may hold values from -0.125 to 0.125
- request_span: int32 [4, 32], replicated, may hold values from 8 to 32
- passage_span: int32 [4, 32], replicated, may hold values from 32 to 64
- matching_pair: int32 [4, 32], replicated, may hold values from 0 to 31, each once within a row
- steepness_pair: float32 [2], replicated, may hold values from 8 to 400
Outputs:
- grad_hidden: bfloat16 [4, 32, 96, 2048], P('section', 'dp')
- pair_loss: float32 [4, 32], P('section', 'dp')
Inputs may be any that keep to these rules, and one draw needn't show every extreme that they name: Each matching_pair[m] names every pair of the micro-batch once.
All inputs are finite; a program needn't handle non-finite values.
Results may differ from a plain program's by a relative error of at most 0.006.
The roundings to bfloat16 on the way count: a program that leaves them out, or rounds other values in their place, can miss the bound.
Values may be sent and summed in bfloat16 or wider, within the bound.
A program may use at most 64 MiB of HBM per device.

v0:
```python
import math

import jax
import jax.numpy as jnp
from jax import lax
from jax.sharding import PartitionSpec as P

QLEN = 32
DLEN = 64


EPSILON = 1e-06
OBJECTIVE_FACTOR = 1024.0
MASKED = -1e30


def head_forward(token_rows, rescale_factor, embedding_matrix):
    values = token_rows.astype(jnp.float32)
    inverse_rms = lax.rsqrt(jnp.mean(values * values, axis=-1, keepdims=True) + EPSILON)
    normed = (values * inverse_rms * rescale_factor).astype(jnp.bfloat16)
    projected = jnp.dot(normed, embedding_matrix, preferred_element_type=jnp.float32)
    inverse_length = lax.rsqrt(jnp.sum(projected * projected, axis=-1, keepdims=True) + EPSILON)
    vectors = (projected * inverse_length).astype(jnp.bfloat16)
    return (vectors, projected, inverse_length, inverse_rms)


def head_backward(
    token_rows,
    rescale_factor,
    embedding_matrix,
    projected,
    inverse_length,
    inverse_rms,
    grad_vectors,
):
    unit = projected * inverse_length
    along = jnp.sum(unit * grad_vectors, axis=-1, keepdims=True)
    grad_projected = (inverse_length * (grad_vectors - unit * along)).astype(jnp.bfloat16)
    grad_normed = lax.dot_general(
        grad_projected,
        embedding_matrix,
        (((1,), (1,)), ((), ())),
        preferred_element_type=jnp.float32,
    )
    values = token_rows.astype(jnp.float32)
    weighted = grad_normed * rescale_factor
    mean_term = jnp.mean(values * weighted, axis=-1, keepdims=True)
    grad_rows = (
        inverse_rms * weighted - values * (inverse_rms * inverse_rms * inverse_rms) * mean_term
    )
    return grad_rows.astype(jnp.bfloat16)


def pool_tokens(similarity, pooling_steepness, live):
    scaled = jnp.where(live[None], pooling_steepness * similarity, MASKED)
    highest = jnp.max(scaled, axis=2, keepdims=True)
    exponent = jnp.exp(scaled - highest)
    totals = jnp.sum(exponent, axis=2, keepdims=True)
    smooth = (highest[:, :, 0] + jnp.log(totals[:, :, 0])) / pooling_steepness
    return (smooth, exponent / totals)


def versus_term(relevance_matrix, matching_pair, logit_multiplier):
    unnormalized_odds = logit_multiplier * relevance_matrix
    highest = jnp.max(unnormalized_odds, axis=1, keepdims=True)
    log_total = highest[:, 0] + jnp.log(jnp.sum(jnp.exp(unnormalized_odds - highest), axis=1))
    columns = jnp.arange(relevance_matrix.shape[1], dtype=jnp.int32)
    correct_label = (columns[None, :] == matching_pair[:, None]).astype(jnp.float32)
    objective_value = log_total - jnp.sum(unnormalized_odds * correct_label, axis=1)
    probability_share = jnp.exp(unnormalized_odds - log_total[:, None])
    score_slope = OBJECTIVE_FACTOR * logit_multiplier * (probability_share - correct_label)
    return (objective_value, score_slope)


def query_weights(request_span, count):
    places = jnp.arange(count, dtype=jnp.int32)
    ones = jnp.where(places[None, :] < request_span[:, None], 1.0, 0.0).astype(jnp.float32)
    return ones / request_span[:, None].astype(jnp.float32)


def live_tokens(passage_span, count):
    places = jnp.arange(count, dtype=jnp.int32)
    return places[None, :] < passage_span[:, None]


def own_rows_pass(query_rows, own_weights, documents, live_all, pooling_steepness):
    pairs = own_weights.shape[0]
    features = query_rows.shape[1]
    total_pairs = documents.shape[0]
    group = math.gcd(total_pairs, max(1, 2048 // DLEN))
    blocks = total_pairs // group

    def block_similarity(start, count):
        docs_block = lax.dynamic_slice_in_dim(documents, start, count, 0).reshape(
            count * DLEN, features
        )
        live_block = lax.dynamic_slice_in_dim(live_all, start, count, 0)
        similarity = lax.dot_general(
            query_rows, docs_block, (((1,), (1,)), ((), ())), preferred_element_type=jnp.float32
        )
        return (similarity.reshape(pairs * QLEN, count, DLEN), live_block, docs_block)

    def forward_pass(index):
        similarity, live_block, _ = block_similarity(index * group, group)
        smooth, _ = pool_tokens(similarity, pooling_steepness, live_block)
        return jnp.sum(smooth.reshape(pairs, QLEN, group) * own_weights[:, :, None], axis=1)

    block_ids = jnp.arange(blocks, dtype=jnp.int32)
    relevance_matrix = lax.map(forward_pass, block_ids)
    relevance_matrix = jnp.transpose(relevance_matrix, (1, 0, 2)).reshape(pairs, total_pairs)
    return (relevance_matrix, block_similarity, group, block_ids)


def own_query_grads(
    query_rows, own_weights, score_slope, block_similarity, group, block_ids, pooling_steepness
):
    pairs = own_weights.shape[0]
    features = query_rows.shape[1]

    def gradient_block(start, count):
        similarity, live_block, docs_block = block_similarity(start, count)
        _, token_weight = pool_tokens(similarity, pooling_steepness, live_block)
        grad_block = lax.dynamic_slice_in_dim(score_slope, start, count, 1)
        coefficient = (own_weights[:, :, None] * grad_block[:, None, :]).reshape(
            pairs * QLEN, count
        )
        similarity_gradient = (coefficient[:, :, None] * token_weight).astype(jnp.bfloat16)
        return (similarity_gradient.reshape(pairs * QLEN, count * DLEN), docs_block)

    def query_step(carry, index):
        similarity_gradient, docs_block = gradient_block(index * group, group)
        return (
            carry + jnp.dot(similarity_gradient, docs_block, preferred_element_type=jnp.float32),
            None,
        )

    grad_queries, _ = lax.scan(
        query_step, jnp.zeros((pairs * QLEN, features), jnp.float32), block_ids
    )
    return (grad_queries, gradient_block)


def own_doc_pass(queries, doc_rows, weights_all, own_live, grad_columns, pooling_steepness):
    total_pairs = queries.shape[0]
    features = doc_rows.shape[1]
    pairs = own_live.shape[0]
    group = math.gcd(total_pairs, max(1, 1024 // QLEN))
    blocks = total_pairs // group

    def block_similarity(index):
        query_block = lax.dynamic_slice_in_dim(queries, index * group, group, 0).reshape(
            group * QLEN, features
        )
        similarity = lax.dot_general(
            query_block, doc_rows, (((1,), (1,)), ((), ())), preferred_element_type=jnp.float32
        )
        block_weight = lax.dynamic_slice_in_dim(weights_all, index * group, group, 0)
        return (similarity.reshape(group * QLEN, pairs, DLEN), block_weight, query_block)

    def backward(carry, index):
        similarity, block_weight, query_block = block_similarity(index)
        _, token_weight = pool_tokens(similarity, pooling_steepness, own_live)
        grad_block = lax.dynamic_slice_in_dim(grad_columns, index * group, group, 0)
        coefficient = (block_weight[:, :, None] * grad_block[:, None, :]).reshape(
            group * QLEN, pairs
        )
        similarity_gradient = (
            (coefficient[:, :, None] * token_weight)
            .astype(jnp.bfloat16)
            .reshape(group * QLEN, pairs * DLEN)
        )
        carry = carry + lax.dot_general(
            similarity_gradient,
            query_block,
            (((0,), (0,)), ((), ())),
            preferred_element_type=jnp.float32,
        )
        return (carry, None)

    block_ids = jnp.arange(blocks, dtype=jnp.int32)
    return (block_similarity, block_ids, group, backward)


def with_both(
    own_queries,
    own_docs,
    weights_all,
    live_all,
    selected_entry,
    first,
    pooling_steepness,
    logit_multiplier,
):
    pairs = own_queries.shape[0]
    features = own_queries.shape[2]
    queries, documents = (
        lax.all_gather(own_queries, "dp", axis=0, tiled=True),
        lax.all_gather(own_docs, "dp", axis=0, tiled=True),
    )
    query_rows = own_queries.reshape(pairs * QLEN, features)
    doc_rows = own_docs.reshape(pairs * DLEN, features)
    own_weights = lax.dynamic_slice_in_dim(weights_all, first, pairs, 0)
    own_live = lax.dynamic_slice_in_dim(live_all, first, pairs, 0)
    relevance_matrix, block_similarity, group, block_ids = own_rows_pass(
        query_rows, own_weights, documents, live_all, pooling_steepness
    )
    all_scores = lax.all_gather(relevance_matrix, "dp", axis=0, tiled=True)
    loss_all, grad_all = versus_term(all_scores, selected_entry, logit_multiplier)
    objective_value = lax.dynamic_slice_in_dim(loss_all, first, pairs, 0)
    grad_rows = lax.dynamic_slice_in_dim(grad_all, first, pairs, 0)
    grad_columns = lax.dynamic_slice_in_dim(grad_all, first, pairs, 1)
    grad_queries, _ = own_query_grads(
        query_rows, own_weights, grad_rows, block_similarity, group, block_ids, pooling_steepness
    )
    _, doc_block_ids, _, backward = own_doc_pass(
        queries, doc_rows, weights_all, own_live, grad_columns, pooling_steepness
    )
    grad_docs, _ = lax.scan(
        backward, jnp.zeros((pairs * DLEN, features), jnp.float32), doc_block_ids
    )
    return (
        grad_queries.reshape(pairs, QLEN, features),
        grad_docs.reshape(pairs, DLEN, features),
        objective_value,
    )


def local(
    latent_states,
    rescale_factor,
    embedding_matrix,
    request_span,
    passage_span,
    matching_pair,
    steepness_pair,
):
    full_proj = lax.all_gather(embedding_matrix, "section", axis=0, tiled=True)
    batch = lax.axis_index("section")
    pairs = latent_states.shape[1]
    length = latent_states.shape[2]
    width = latent_states.shape[3]
    first = lax.axis_index("dp") * pairs
    pooling_steepness = steepness_pair[0]
    logit_multiplier = steepness_pair[1]
    request_spans = lax.dynamic_index_in_dim(request_span, batch, 0, keepdims=False)
    passage_spans = lax.dynamic_index_in_dim(passage_span, batch, 0, keepdims=False)
    selected_entry = lax.dynamic_index_in_dim(matching_pair, batch, 0, keepdims=False)
    weights_all = query_weights(request_spans, QLEN)
    live_all = live_tokens(passage_spans, DLEN)
    flat_rows = latent_states.reshape(pairs * length, width)
    vectors, projected, inverse_length, inverse_rms = head_forward(
        flat_rows, rescale_factor, full_proj
    )
    vectors = vectors.reshape(pairs, length, -1)
    features = vectors.shape[2]
    own_queries = vectors[:, :QLEN]
    own_docs = vectors[:, QLEN:]
    grad_queries, grad_docs, objective_value = with_both(
        own_queries,
        own_docs,
        weights_all,
        live_all,
        selected_entry,
        first,
        pooling_steepness,
        logit_multiplier,
    )
    grad_vectors = jnp.concatenate([grad_queries, grad_docs], axis=1).reshape(
        pairs * length, features
    )
    grad_rows = head_backward(
        flat_rows, rescale_factor, full_proj, projected, inverse_length, inverse_rms, grad_vectors
    )
    return (grad_rows.reshape(1, pairs, length, width), objective_value[None, :])


def solution(mesh):
    return jax.shard_map(
        local,
        mesh=mesh,
        in_specs=(P("section", "dp", None, None), P(), P("section", None), P(), P(), P(), P()),
        out_specs=(P("section", "dp", None, None), P("section", "dp")),
        check_vma=False,
    )
```

profile of v0, /device:TPU:0, one launch (start us, length us, event | category | flops | bytes accessed | tf_op | source)
XLA Modules:
  0.0 135.8 jit_solution(408165753325786143)
XLA Ops:
  1.3 1.2 fusion.34
  2.5 1.3 fusion.36
  4.5 1.8 %fusion.2 = f32[4,96]{1,0:T(4,128)S(1)} fusion(bf16[1,4,96,2048]{3,2,1,0:T(8,128)(2,1)} %param.7), kind=kLoop, calls=%fused_computation.6 | loop fusion | flops 2358912 | bytes 1574400 | tf_op jit(solution)/shard_map/reduce_sum | solution.py:19
  9.0 8.8 %all_gather.12 = bf16[2048,128]{1,0:T(8,128)(2,1)S(1)} all-gather(bf16[512,128]{1,0:T(8,128)(2,1)} %param.9), channel_id=1, replica_groups=mesh['section'=4,'dp'=8] {'section'}, dimensions={0}, use_global_device_ids=true | all-gather | bytes 655360 | tf_op jit(solution)/shard_map/all_gather | solution.py:237
  17.8 1.1 fusion.4
  19.8 33.1 %all_gather.15 = bf16[32,32,128]{2,1,0:T(8,128)(2,1)} all-gather(bf16[4,32,128]{2,1,0:T(8,128)(2,1)S(1)} %slice.16), channel_id=1, replica_groups=mesh['section'=4,'dp'=8] {'dp'}, dimensions={0}, use_global_device_ids=true | all-gather | bytes 294912 | tf_op jit(solution)/shard_map/all_gather | solution.py:197
  52.9 31.2 %all_gather.13 = bf16[32,64,128]{2,1,0:T(8,128)(2,1)S(1)} all-gather(bf16[4,64,128]{2,1,0:T(8,128)(2,1)S(1)} %slice.17), channel_id=1, replica_groups=mesh['section'=4,'dp'=8] {'dp'}, dimensions={0}, use_global_device_ids=true | all-gather | bytes 589824 | tf_op jit(solution)/shard_map/all_gather | solution.py:198
  84.1 0.8 copy-done.2
  84.9 1.2 fusion.37
  86.3 1.3 add_divide_fusion
  87.6 0.8 div.62
  88.4 0.7 multiply_reduce_fusion.1
  89.1 0.8 copy.15
  89.9 26.1 %all-gather = f32[8,4,32]{2,1,0:T(4,128)S(1)} all-gather(f32[1,4,32]{2,1,0:T(4,128)S(1)} %bitcast.82), channel_id=1, replica_groups=mesh['section'=4,'dp'=8] {'dp'}, dimensions={0}, use_global_device_ids=true | all-gather | bytes 4608 | tf_op jit(solution)/shard_map/all_gather | solution.py:207
  116.0 0.7 fusion.33
  116.9 0.8 select_reduce_fusion
  119.8 0.8 mul.254
  121.3 0.7 broadcast_multiply_fusion.2
  122.0 1.1 multiply_convert_fusion
  123.9 3.2 %fusion.17 = f32[4,64,128]{2,1,0:T(8,128)} fusion(bf16[1024,128,1]{1,0,2:T(8,128)(2,1)} %bitcast.79, f32[1024,4]{0,1:T(4,128)S(1)} %broadcast_multiply_fusion.1, f32[]{:T(128)} %bitcast.4, pred[4,64]{1,0:T(4,128)(4,1)} %constant_dynamic-slice_fusion, bf16[4,96,128]{2,1,0:T(8,128)(2,1)S(1)} %bitcast.77), kind=kOutput, calls=%fused_computation.24 | convolution fusion | flops 135798912 | bytes 738304 | tf_op jit(solution)/shard_map/while/body/eval_jaxpr/dot_general | solution.py:172
  127.1 2.5 %copy.17 = bf16[128,32,64]{2,1,0:T(8,128)(2,1)} copy(bf16[128,32,64]{0,2,1:T(8,128)(2,1)S(1)} %copy-done.4) | data formatting | bytes 1048576 | tf_op jit(solution)/shard_map/while/body/eval_jaxpr/convert_element_type | solution.py:127
  129.6 2.0 %dot_general.32 = bf16[4,32,2048]{2,1,0:T(8,128)(2,1)S(1)} reshape(bf16[128,32,64]{2,1,0:T(8,128)(2,1)} %copy.17) | data formatting | bytes 1048576 | tf_op jit(solution)/shard_map/while/body/eval_jaxpr/dot_general | solution.py:133
  132.0 0.9 pad_maximum_fusion
  134.0 1.8 %fusion.7 = bf16[384,2048]{1,0:T(8,128)(2,1)} fusion(bf16[1,4,96,2048]{3,2,1,0:T(8,128)(2,1)S(1)} %copy-done.1, f32[384,2048]{1,0:T(8,128)S(1)} %get-tuple-element.78, f32[384]{0:T(512)S(1)} %broadcast_multiply_fusion.3, f32[384]{0:T(512)S(1)} %copy-done.6, f32[384]{0:T(512)S(1)} %rsqrt.23), kind=kLoop, calls=%fused_computation.11 | loop fusion | flops 4718592 | bytes 6296064 | tf_op jit(solution)/shard_map/convert_element_type | solution.py:51
  (46 shorter events, 9.6 us)
Async XLA Ops:
  0.6 0.7 copy-start
  0.6 17.2 %copy-start.1 = (bf16[1,4,96,2048]{3,2,1,0:T(8,128)(2,1)S(1)}, bf16[1,4,96,2048]{3,2,1,0:T(8,128)(2,1)}, u32[]{:S(2)}) copy-start(bf16[1,4,96,2048]{3,2,1,0:T(8,128)(2,1)} %param.7) | copy-start | bytes 4718596
  84.1 0.8 copy-start.2
  123.1 4.0 %copy-start.4 = (bf16[128,32,64]{0,2,1:T(8,128)(2,1)S(1)}, bf16[128,32,64]{0,2,1:T(8,128)(2,1)}, u32[]{:S(2)}) copy-start(bf16[128,32,64]{0,2,1:T(8,128)(2,1)} %multiply_convert_fusion) | copy-start | bytes 1572868
  123.9 7.7 %copy-start.3 = (bf16[32,64,128]{2,1,0:T(8,128)(2,1)S(1)}, bf16[32,64,128]{2,1,0:T(8,128)(2,1)}, u32[]{:S(2)}) copy-start(bf16[32,64,128]{2,1,0:T(8,128)(2,1)} %copy-done.2) | copy-start | bytes 1572868
  127.1 6.2 %copy-start.5 = (f32[2048]{0:T(1024)S(1)}, f32[2048]{0:T(1024)}, u32[]{:S(2)}) copy-start(f32[2048]{0:T(1024)} %param.8) | copy-start | bytes 24580
  132.9 1.1 copy-start.6
where the time goes:
time: 137 us; the launch traced here: 136 us
  blocking collectives  99.2 us (72%)
  other arithmetic  15 us (11%)
  local copies, waits for them, and re-layouts  14.1 us (10%)
  matrix products  6.05 us (4%)
  between operations  1.46 us (1%)
    all_gather x1, blocking collectives, with_both(): lax.all_gather(own_queries, 'dp', axis=0, tiled=True)  33.1 us
    all_gather x1, blocking collectives, with_both(): lax.all_gather(own_docs, 'dp', axis=0, tiled=True)  31.2 us
    all_gather x1, blocking collectives, with_both(): all_scores = lax.all_gather(relevance_matrix, 'dp', axis=0, tiled=True)  26.1 us
    all_gather x1, blocking collectives, local(): full_proj = lax.all_gather(embedding_matrix, 'section', axis=0, tiled=True)  8.84 us
    dot_general x1, matrix products, backward(): lax.dot_general(similarity_gradient, query_block, (((0,), (0,)), ((), ())...  3.16 us

commit v1 on v0

v1 whole, which is shorter than its diff:
```python
import functools

import jax
import jax.numpy as jnp
from jax import lax
from jax.experimental import pallas as pl
from jax.experimental.pallas import tpu as pltpu
from jax.sharding import PartitionSpec as P

QLEN = 32
DLEN = 64

EPSILON = 1e-06
OBJECTIVE_FACTOR = 1024.0
MASKED = -1e30

ROWS = 16
CHUNKS = 2


def dot(a, b, dims, precision=None):
    return lax.dot_general(
        a, b, (dims, ((), ())), precision=precision, preferred_element_type=jnp.float32
    )


def body(
    n,
    sections,
    x_hbm,
    gain_ref,
    w_hbm,
    request_ref,
    passage_ref,
    match_ref,
    steep_ref,
    out_hbm,
    loss_ref,
    xbuf,
    nrm,
    wbuf,
    proj,
    qinv,
    rinv,
    docs,
    queries,
    e_own,
    e_all,
    gbuf,
    gqbuf,
    gnbuf,
    obuf,
    smooth_own,
    tinv_own,
    smooth_all,
    tinv_all,
    label_own,
    label_all,
    weight_all,
    lse_buf,
    x_sem,
    w_sem,
    wsend,
    wrecv,
    dsend,
    drecv,
    qsend,
    qrecv,
    lsend,
    lrecv,
    osem,
):
    pairs, length, width = xbuf.shape
    depth = wbuf.shape[1]
    lanes = pairs * QLEN
    section = lax.axis_index("section")
    me = lax.axis_index("dp")

    half = n // 2
    col = me % 2
    pos = (me // 2) * (1 - col) + (n - 1 - me // 2) * col

    def device_at(p):
        side = p // half
        return 2 * (p * (1 - side) + (n - 1 - p) * side) + side

    def owner_of(slot):
        return device_at((pos + n - slot) % n)

    right = device_at((pos + 1) % n)
    left = device_at((pos + n - 1) % n)

    chips = sections // 2
    core = section % 2
    chip = section // 2
    partner = chip * 2 + 1 - core

    def over(t):
        return ((chip + t) % chips) * 2 + core

    def remote(src, dst, send, recv, axis, index):
        return pltpu.make_async_remote_copy(
            src_ref=src,
            dst_ref=dst,
            send_sem=send,
            recv_sem=recv,
            device_id={axis: index},
            device_id_type=pl.DeviceIdType.MESH,
        )

    x_copies = [
        pltpu.make_async_copy(x_hbm.at[0, b], xbuf.at[b], x_sem.at[b]) for b in range(pairs)
    ]
    w_copy = pltpu.make_async_copy(w_hbm, wbuf.at[section], w_sem)
    w_copy.start()
    for copy in x_copies:
        copy.start()

    barrier = pltpu.get_barrier_semaphore()
    greeted = [("section", partner)]
    greeted += [("section", over(t)) for t in range(1, chips)]
    greeted += [("dp", right), ("dp", left)]
    for axis, index in greeted:
        pl.semaphore_signal(
            barrier, inc=1, device_id={axis: index}, device_id_type=pl.DeviceIdType.MESH
        )
    pl.semaphore_wait(barrier, len(greeted))

    part = depth // CHUNKS
    started = []

    def launch(copy):
        copy.start()
        started.append(copy)

    def piece(ref, index, h):
        return ref.at[index, pl.ds(h * part, part)]

    for t in range(1, chips):
        for h in range(CHUNKS):
            launch(
                remote(
                    w_hbm.at[pl.ds(h * part, part)],
                    piece(wbuf, section, h),
                    wsend.at[t, h],
                    wrecv.at[t, h],
                    "section",
                    over(t),
                )
            )
    for h in range(CHUNKS):
        launch(
            remote(
                w_hbm.at[pl.ds(h * part, part)],
                piece(wbuf, section, h),
                wsend.at[0, h],
                wrecv.at[0, h],
                "section",
                partner,
            )
        )

    gain = gain_ref[...]
    for b in range(pairs):
        x_copies[b].wait()

        def norm_rows(i, carry, b=b):
            r = pl.multiple_of(i * ROWS, ROWS)
            v = xbuf[b, pl.ds(r, ROWS), :].astype(jnp.float32)
            q = lax.rsqrt(jnp.sum(v * v, axis=1, keepdims=True) * (1.0 / width) + EPSILON)
            full = pl.multiple_of(b * length + i * ROWS, ROWS)
            qinv[pl.ds(full, ROWS), :] = jnp.broadcast_to(q, (ROWS, 128))
            z = (v * q * gain).astype(jnp.bfloat16)
            for k in range(sections):
                nrm[k, pl.ds(full, ROWS), :] = z[:, k * depth : (k + 1) * depth]
            return carry

        lax.fori_loop(0, length // ROWS, norm_rows, 0, unroll=2)

    def add_piece(index, first=False):
        term = dot(nrm[index], wbuf[index], ((1,), (0,)))
        proj[...] = term if first else proj[...] + term

    w_copy.wait()
    add_piece(section, True)
    for h in range(CHUNKS):
        place = piece(wbuf, partner, h)
        remote(place, place, wsend.at[0, h], wrecv.at[0, h], "section", partner).wait_recv()
    add_piece(partner)
    for t in range(1, chips):
        source = over(chips - t)
        for h in range(CHUNKS):
            place = piece(wbuf, source, h)
            remote(place, place, wsend.at[t, h], wrecv.at[t, h], "section", partner).wait_recv()
            launch(
                remote(
                    place,
                    place,
                    wsend.at[chips + t, h],
                    wrecv.at[chips + t, h],
                    "section",
                    partner,
                )
            )
        add_piece(source)
    for t in range(1, chips):
        source = ((chip + chips - t) % chips) * 2 + 1 - core
        for h in range(CHUNKS):
            place = piece(wbuf, source, h)
            remote(
                place, place, wsend.at[chips + t, h], wrecv.at[chips + t, h], "section", partner
            ).wait_recv()
        add_piece(source)

    for b in range(pairs):
        p = proj[b * length : (b + 1) * length, :]
        r = lax.rsqrt(jnp.sum(p * p, axis=1, keepdims=True) + EPSILON)
        rinv[b * length : (b + 1) * length, :] = jnp.broadcast_to(r, p.shape)
        v = (p * r).astype(jnp.bfloat16)
        queries[0, b * QLEN : (b + 1) * QLEN, :] = v[:QLEN]
        docs[0, b * DLEN : (b + 1) * DLEN, :] = v[QLEN:]

    def onward(buf, send, recv, slot, ascending):
        to = slot + 1 if ascending else (n if slot == 0 else slot) - 1
        return remote(
            buf.at[slot],
            buf.at[to],
            send.at[0 if ascending else 1, slot],
            recv.at[to],
            "dp",
            right if ascending else left,
        )

    chains = [
        (docs, dsend, drecv, True, n // 2),
        (docs, dsend, drecv, False, n - 1 - n // 2),
        (queries, qsend, qrecv, True, n - 1 - n // 2),
        (queries, qsend, qrecv, False, n // 2),
    ]
    for buf, send, recv, ascending, reach in chains:
        if reach > 0:
            launch(onward(buf, send, recv, 0, ascending))

    beta = steep_ref[0]
    sharp = steep_ref[1]
    inverse_beta = 1.0 / jnp.full((1, lanes), beta, jnp.float32)
    place_j = lax.broadcasted_iota(jnp.int32, (DLEN, lanes), 0)
    lane = lax.broadcasted_iota(jnp.int32, (1, lanes), 1)
    lane_pair = lane // QLEN
    lane_token = lane % QLEN

    def spread(ref, first):
        value = jnp.full((1, lanes), ref[section, first], jnp.int32)
        for b in range(1, pairs):
            value = jnp.where(lane_pair == b, ref[section, first + b], value)
        return value

    def weights_of(owner):
        span = spread(request_ref, owner * pairs)
        return jnp.where(lane_token < span, 1.0 / span.astype(jnp.float32), 0.0)

    def forward(doc_rows, query_rows, owner, slot, e_ref, smooth_ref, tinv_ref):
        s = dot(doc_rows, query_rows, ((1,), (1,)))
        for c in range(pairs):
            span = passage_ref[section, owner * pairs + c]
            sc = jnp.where(place_j < span, beta * s[c * DLEN : (c + 1) * DLEN], MASKED)
            high = jnp.max(sc, axis=0, keepdims=True)
            e = jnp.exp(sc - high)
            total = jnp.sum(e, axis=0, keepdims=True)
            e_ref[slot, c * DLEN : (c + 1) * DLEN, :] = e
            row = slot * pairs + c
            smooth_ref[row : row + 1, :] = (high + jnp.log(total)) * inverse_beta
            tinv_ref[row : row + 1, :] = 1.0 / total

    own_weight = weights_of(me)
    own_match = spread(match_ref, me * pairs)

    def own_forward(slot):
        owner = owner_of(slot)
        forward(docs[slot], queries[0], owner, slot, e_own, smooth_own, tinv_own)
        for c in range(pairs):
            row = slot * pairs + c
            label_own[row : row + 1, :] = jnp.where(own_match == owner * pairs + c, 1.0, 0.0)

    own_forward(0)
    for slot in range(n):
        owner = owner_of(slot)
        match = spread(match_ref, owner * pairs)
        weight = weights_of(owner)
        for c in range(pairs):
            row = slot * pairs + c
            label_all[row : row + 1, :] = jnp.where(match == me * pairs + c, 1.0, 0.0)
            weight_all[row : row + 1, :] = weight
    for d in range(1, n // 2 + 1):
        for buf, send, recv, ascending, reach in chains:
            if reach >= d:
                slot = d if ascending else n - d
                place = buf.at[slot]
                remote(place, place, send.at[0, 0], recv.at[slot], "dp", right).wait_recv()
                if reach > d:
                    launch(onward(buf, send, recv, slot, ascending))
        for slot in sorted({d, n - d}):
            own_forward(slot)

    from_lane = lax.broadcasted_iota(jnp.int32, (lanes, lanes), 0) // QLEN
    to_lane = lax.broadcasted_iota(jnp.int32, (lanes, lanes), 1) // QLEN
    same = jnp.where(from_lane == to_lane, 1.0, 0.0)
    highest = lax.Precision.HIGHEST
    scores = dot(smooth_own[...] * own_weight, same, ((1,), (0,)), highest)
    logits = sharp * scores
    high = jnp.max(logits, axis=0, keepdims=True)
    lse = high + jnp.log(jnp.sum(jnp.exp(logits - high), axis=0, keepdims=True))
    lse_buf[0] = jnp.broadcast_to(lse, (8, lanes))
    for k in range(1, n):
        launch(
            remote(
                lse_buf.at[0],
                lse_buf.at[k],
                lsend.at[k],
                lrecv.at[k],
                "dp",
                device_at((pos + k) % n),
            )
        )
    label = label_own[...]
    loss = lse - jnp.sum(logits * label, axis=0, keepdims=True)
    for b in range(pairs):
        loss_ref[:, b : b + 1] = loss[:, b * QLEN : b * QLEN + 1]
    slope = OBJECTIVE_FACTOR * sharp * (jnp.exp(logits - lse) - label)
    tinv_own[...] = own_weight * slope * tinv_own[...]

    def grads(slot, e_ref, coefficient_ref):
        for c in range(pairs):
            row = slot * pairs + c
            gbuf[slot, c * DLEN : (c + 1) * DLEN, :] = (
                coefficient_ref[row : row + 1, :] * e_ref[slot, c * DLEN : (c + 1) * DLEN, :]
            ).astype(jnp.bfloat16)

    for slot in range(n):
        grads(slot, e_own, tinv_own)
    grad_query = dot(
        gbuf[...].reshape(n * pairs * DLEN, lanes),
        docs[...].reshape(n * pairs * DLEN, docs.shape[2]),
        ((0,), (0,)),
    )

    all_w = wbuf[...].reshape(sections * depth, wbuf.shape[2])
    out_copies = []

    def head_backward(gradient, first, count):
        for b in range(pairs):
            lo = b * length + first
            g = gradient[b * count : (b + 1) * count]
            r = rinv[lo : lo + count, :]
            u = proj[lo : lo + count, :] * r
            along = jnp.sum(u * g, axis=1, keepdims=True)
            gqbuf[b * count : (b + 1) * count, :] = (r * (g - u * along)).astype(jnp.bfloat16)
        gnbuf[0 : pairs * count, :] = dot(gqbuf[0 : pairs * count, :], all_w, ((1,), (1,)))
        for b in range(pairs):

            def rows(i, carry, b=b):
                r = pl.multiple_of(first + i * ROWS, ROWS)
                v = xbuf[b, pl.ds(r, ROWS), :].astype(jnp.float32)
                at = pl.multiple_of(b * count + i * ROWS, ROWS)
                weighted = gnbuf[pl.ds(at, ROWS), :] * gain
                mean = jnp.sum(v * weighted, axis=1, keepdims=True) * (1.0 / width)
                full = pl.multiple_of(b * length + first + i * ROWS, ROWS)
                q = qinv[pl.ds(full, ROWS), :][:, 0:1]
                obuf[b, pl.ds(r, ROWS), :] = (q * weighted - v * (q * q * q * mean)).astype(
                    jnp.bfloat16
                )
                return carry

            lax.fori_loop(0, count // ROWS, rows, 0, unroll=2)
            copy = pltpu.make_async_copy(
                obuf.at[b, pl.ds(first, count)],
                out_hbm.at[0, b, pl.ds(first, count)],
                osem.at[0 if first == 0 else 1, b],
            )
            copy.start()
            out_copies.append(copy)

    head_backward(grad_query, 0, QLEN)

    for slot in range(n):
        forward(docs[0], queries[slot], me, slot, e_all, smooth_all, tinv_all)
    weight = weight_all[...]
    logits = sharp * dot(smooth_all[...] * weight, same, ((1,), (0,)), highest)
    smooth_all[...] = logits
    for slot in range(n):
        rows = slice(slot * pairs, (slot + 1) * pairs)
        if slot:
            place = lse_buf.at[slot]
            remote(place, place, lsend.at[slot], lrecv.at[slot], "dp", right).wait_recv()
        share = jnp.exp(smooth_all[rows, :] - lse_buf[slot][0:1])
        slope = OBJECTIVE_FACTOR * sharp * (share - label_all[rows, :])
        tinv_all[rows, :] = weight_all[rows, :] * slope * tinv_all[rows, :]
    grad_doc = jnp.zeros((pairs * DLEN, docs.shape[2]), jnp.float32)
    for slot in range(n):
        grads(slot, e_all, tinv_all)
        grad_doc = grad_doc + dot(gbuf[slot], queries[slot], ((1,), (0,)))
    head_backward(grad_doc, QLEN, DLEN)

    for copy in started:
        copy.wait_send()
    for copy in out_copies:
        copy.wait()


def local(
    n,
    sections,
    latent_states,
    rescale_factor,
    embedding_matrix,
    request_span,
    passage_span,
    matching_pair,
    steepness_pair,
):
    _, pairs, length, width = latent_states.shape
    depth, features = embedding_matrix.shape
    rows = pairs * length
    lanes = pairs * QLEN
    f32, bf16 = jnp.float32, jnp.bfloat16
    dma = pltpu.SemaphoreType.DMA
    vmem = pl.BlockSpec(memory_space=pltpu.VMEM)
    smem = pl.BlockSpec(memory_space=pltpu.SMEM)
    anywhere = pl.BlockSpec(memory_space=pl.ANY)
    chips = sections // 2
    return pl.pallas_call(
        functools.partial(body, n, sections),
        out_shape=(
            jax.ShapeDtypeStruct(latent_states.shape, bf16),
            jax.ShapeDtypeStruct((1, pairs), f32),
        ),
        in_specs=[anywhere, vmem, anywhere, smem, smem, smem, smem],
        out_specs=(anywhere, vmem),
        scratch_shapes=[
            pltpu.VMEM((pairs, length, width), bf16),
            pltpu.VMEM((sections, rows, depth), bf16),
            pltpu.VMEM((sections, depth, features), bf16),
            pltpu.VMEM((rows, features), f32),
            pltpu.VMEM((rows, 128), f32),
            pltpu.VMEM((rows, features), f32),
            pltpu.VMEM((n, pairs * DLEN, features), bf16),
            pltpu.VMEM((n, pairs * QLEN, features), bf16),
            pltpu.VMEM((n, pairs * DLEN, lanes), f32),
            pltpu.VMEM((n, pairs * DLEN, lanes), f32),
            pltpu.VMEM((n, pairs * DLEN, lanes), bf16),
            pltpu.VMEM((pairs * DLEN, features), bf16),
            pltpu.VMEM((pairs * DLEN, width), f32),
            pltpu.VMEM((pairs, length, width), bf16),
            pltpu.VMEM((n * pairs, lanes), f32),
            pltpu.VMEM((n * pairs, lanes), f32),
            pltpu.VMEM((n * pairs, lanes), f32),
            pltpu.VMEM((n * pairs, lanes), f32),
            pltpu.VMEM((n * pairs, lanes), f32),
            pltpu.VMEM((n * pairs, lanes), f32),
            pltpu.VMEM((n * pairs, lanes), f32),
            pltpu.VMEM((n, 8, lanes), f32),
            dma((pairs,)),
            dma(()),
            dma((2 * chips, CHUNKS)),
            dma((2 * chips, CHUNKS)),
            dma((2, n)),
            dma((n,)),
            dma((2, n)),
            dma((n,)),
            dma((n,)),
            dma((n,)),
            dma((2, pairs)),
        ],
        compiler_params=pltpu.CompilerParams(
            collective_id=0, has_side_effects=True, vmem_limit_bytes=60 * 1024 * 1024
        ),
        name="late_interaction",
    )(
        latent_states,
        rescale_factor.reshape(1, width),
        embedding_matrix,
        request_span,
        passage_span,
        matching_pair,
        steepness_pair,
    )


def solution(mesh):
    return jax.shard_map(
        functools.partial(local, mesh.shape["dp"], mesh.shape["section"]),
        mesh=mesh,
        in_specs=(P("section", "dp", None, None), P(), P("section", None), P(), P(), P(), P()),
        out_specs=(P("section", "dp", None, None), P("section", "dp")),
        check_vma=False,
    )
```

time: 137 us -> 39 us (0.28)
  blocking collectives: 99.2 us -> 0 us
  Pallas kernels: 0 us -> 35 us
  other arithmetic: 15 us -> 0 us
  local copies, waits for them, and re-layouts: 14.1 us -> 3.24 us
  matrix products: 6.05 us -> 0 us
    all_gather x4 -> x0, blocking collectives: 99.2 us -> none  [the longest x1 33.1 us: with_both(): lax.all_gather(own_queries, 'dp', axis=0, tiled=True)]
    pallas_call x0 -> x1, Pallas kernels: none -> 35 us  [local(): pl.pallas_call(functools.partial(body, n, sections), out_shape=(jax.Shape...]
    dot_general x5 -> x0, matrix products: 6.05 us -> none  [the longest x1 3.16 us: backward(): lax.dot_general(similarity_gradient, query_block, (((0,), (0,)), ((), ())...]
    convert_element_type x6 -> x0, other arithmetic: 5.47 us -> none  [the longest x1 1.8 us: head_backward(): return grad_rows.astype(jnp.bfloat16)]
    reduce_sum x5 -> x0, other arithmetic: 3.72 us -> none  [the longest x1 1.8 us: head_forward(): jnp.mean(values * values, axis=-1, keepdims=True) + EPSILON]
    mul x4 -> x0, other arithmetic: 2.67 us -> none  [the longest x1 0.72 us: gradient_block(): own_weights[:, :, None] * grad_block[:, None, :]]
    convert_element_type x1 -> x0, local copies, waits for them, and re-layouts: 2.52 us -> none  [gradient_block(): (coefficient[:, :, None] * token_weight).astype(jnp.bfloat16)]
    mul x5 -> x0, local copies, waits for them, and re-layouts: 2.3 us -> none  [the longest x3 2.12 us: gradient_block(): own_weights[:, :, None] * grad_block[:, None, :]]
where the time goes in v1:
time: 39 us; the launch traced here: 38.9 us
  Pallas kernels  35 us (90%)
  local copies, waits for them, and re-layouts  3.24 us (8%)
  between operations  0.65 us (2%)
    pallas_call x1, Pallas kernels, local(): pl.pallas_call(functools.partial(body, n, sections), out_shape=(jax.Shape...  35 us
    unnamed x4, local copies, waits for them, and re-layouts  3.24 us

profile of v1, /device:TPU:0, one launch (start us, length us, event | category | flops | bytes accessed | tf_op | source)
XLA Modules:
  0.0 38.9 jit_solution(11723136956487467347)
XLA Ops:
  0.6 35.0 %late_interaction.1 = (bf16[1,4,96,2048]{3,2,1,0:T(8,128)(2,1)}, f32[1,4]{1,0:T(1,128)}) custom-call(bf16[1,4,96,2048]{3,2,1,0:T(8,128)(2,1)} %x_hbm.1, f32[1,2048]{1,0:T(1,128)} %bitcast.1, bf16[512,128]{1,0:T(8,128)(2,1)} %w_hbm.1, s32[4,32]{1,0:T(4,128)} %request_ref.1, s32[4,32]{1,0:T(4,128)} %passage_ref.1, s32[4,32]{1,0:T(4,128)} %match_ref.1, f32[2]{0:T(128)} %steep_ref.1), custom_call_target="tpu_custom_call" | custom-call | tf_op jit(solution)/shard_map/late_interaction/pallas_call | solution.py:431
  35.6 0.0 copy-start
  35.6 2.7 %copy.11 = bf16[1,4,96,2048]{3,2,1,0:T(8,128)(2,1)} copy(bf16[1,4,96,2048]{3,2,1,0:T(8,128)(2,1)} %get-tuple-element.4) | data formatting | bytes 3145728
  38.3 0.0 copy-done
  38.3 0.5 %copy.12 = f32[1,4]{1,0:T(1,128)} copy(f32[1,4]{1,0:T(1,128)S(1)} %copy-done) | data formatting | bytes 32
Async XLA Ops:
  35.6 2.7 %copy-start = (f32[1,4]{1,0:T(1,128)S(1)}, f32[1,4]{1,0:T(1,128)}, u32[]{:S(2)}) copy-start(f32[1,4]{1,0:T(1,128)} %get-tuple-element.5) | copy-start | bytes 52

commit v2 on v1

--- a/solution.py
+++ b/solution.py
@@ -15,7 +15,9 @@
 MASKED = -1e30
 
 ROWS = 16
-CHUNKS = 2
+CHUNKS = 4
+QUERY_CHUNKS = 2
+DOC_CHUNKS = 4
 
 
 def dot(a, b, dims, precision=None):
@@ -220,26 +222,46 @@
         queries[0, b * QLEN : (b + 1) * QLEN, :] = v[:QLEN]
         docs[0, b * DLEN : (b + 1) * DLEN, :] = v[QLEN:]
 
-    def onward(buf, send, recv, slot, ascending):
+    def chunk(buf, slot, h, count):
+        size = buf.shape[1] // count
+        return buf.at[slot, pl.ds(h * size, size)]
+
+    def onward(chain, slot, h):
+        buf, send, recv, ascending, _, count = chain
         to = slot + 1 if ascending else (n if slot == 0 else slot) - 1
         return remote(
-            buf.at[slot],
-            buf.at[to],
-            send.at[0 if ascending else 1, slot],
-            recv.at[to],
+            chunk(buf, slot, h, count),
+            chunk(buf, to, h, count),
+            send.at[0 if ascending else 1, slot, h],
+            recv.at[to, h],
             "dp",
             right if ascending else left,
         )
 
-    chains = [
-        (docs, dsend, drecv, True, n // 2),
-        (docs, dsend, drecv, False, n - 1 - n // 2),
-        (queries, qsend, qrecv, True, n - 1 - n // 2),
-        (queries, qsend, qrecv, False, n // 2),
+    query_chains = [
+        (queries, qsend, qrecv, True, n // 2, QUERY_CHUNKS),
+        (queries, qsend, qrecv, False, n - 1 - n // 2, QUERY_CHUNKS),
     ]
-    for buf, send, recv, ascending, reach in chains:
-        if reach > 0:
-            launch(onward(buf, send, recv, 0, ascending))
+    doc_chains = [
+        (docs, dsend, drecv, True, n - 1 - n // 2, DOC_CHUNKS),
+        (docs, dsend, drecv, False, n // 2, DOC_CHUNKS),
+    ]
+
+    def pass_on(chains, d):
+        for h in range(chains[0][5]):
+            for chain in chains:
+                buf, send, recv, ascending, reach, count = chain
+                if d > 0 and reach >= d:
+                    slot = d if ascending else n - d
+                    place = chunk(buf, slot, h, count)
+                    remote(
+                        place, place, send.at[0, 0, h], recv.at[slot, h], "dp", right
+                    ).wait_recv()
+                if reach > d:
+                    launch(onward(chain, d if ascending else (n - d) % n, h))
+
+    pass_on(query_chains, 0)
+    pass_on(doc_chains, 0)
 
     beta = steep_ref[0]
     sharp = steep_ref[1]
@@ -282,6 +304,10 @@
             row = slot * pairs + c
             label_own[row : row + 1, :] = jnp.where(own_match == owner * pairs + c, 1.0, 0.0)
 
+    def doc_forward(slot):
+        forward(docs[0], queries[slot], me, slot, e_all, smooth_all, tinv_all)
+
+    doc_forward(0)
     own_forward(0)
     for slot in range(n):
         owner = owner_of(slot)
@@ -291,37 +317,45 @@
             row = slot * pairs + c
             label_all[row : row + 1, :] = jnp.where(match == me * pairs + c, 1.0, 0.0)
             weight_all[row : row + 1, :] = weight
-    for d in range(1, n // 2 + 1):
-        for buf, send, recv, ascending, reach in chains:
-            if reach >= d:
-                slot = d if ascending else n - d
-                place = buf.at[slot]
-                remote(place, place, send.at[0, 0], recv.at[slot], "dp", right).wait_recv()
-                if reach > d:
-                    launch(onward(buf, send, recv, slot, ascending))
-        for slot in sorted({d, n - d}):
-            own_forward(slot)
 
     from_lane = lax.broadcasted_iota(jnp.int32, (lanes, lanes), 0) // QLEN
     to_lane = lax.broadcasted_iota(jnp.int32, (lanes, lanes), 1) // QLEN
     same = jnp.where(from_lane == to_lane, 1.0, 0.0)
     highest = lax.Precision.HIGHEST
+
+    for d in range(1, n // 2 + 1):
+        pass_on(query_chains, d)
+        for slot in sorted({d, n - d}):
+            doc_forward(slot)
+        if d == n // 2:
+            smooth_all[...] = sharp * dot(
+                smooth_all[...] * weight_all[...], same, ((1,), (0,)), highest
+            )
+            for slot in range(n):
+                logits = smooth_all[slot * pairs : (slot + 1) * pairs, :]
+                high = jnp.max(logits, axis=0, keepdims=True)
+                lse_buf[0, slot : slot + 1, :] = high + jnp.log(
+                    jnp.sum(jnp.exp(logits - high), axis=0, keepdims=True)
+                )
+            for k in range(1, n):
+                launch(
+                    remote(
+                        lse_buf.at[0],
+                        lse_buf.at[k],
+                        lsend.at[k],
+                        lrecv.at[k],
+                        "dp",
+                        device_at((pos + k) % n),
+                    )
+                )
+        pass_on(doc_chains, d)
+        for slot in sorted({d, n - d}):
+            own_forward(slot)
+
     scores = dot(smooth_own[...] * own_weight, same, ((1,), (0,)), highest)
     logits = sharp * scores
     high = jnp.max(logits, axis=0, keepdims=True)
     lse = high + jnp.log(jnp.sum(jnp.exp(logits - high), axis=0, keepdims=True))
-    lse_buf[0] = jnp.broadcast_to(lse, (8, lanes))
-    for k in range(1, n):
-        launch(
-            remote(
-                lse_buf.at[0],
-                lse_buf.at[k],
-                lsend.at[k],
-                lrecv.at[k],
-                "dp",
-                device_at((pos + k) % n),
-            )
-        )
     label = label_own[...]
     loss = lse - jnp.sum(logits * label, axis=0, keepdims=True)
     for b in range(pairs):
@@ -382,17 +416,15 @@
 
     head_backward(grad_query, 0, QLEN)
 
-    for slot in range(n):
-        forward(docs[0], queries[slot], me, slot, e_all, smooth_all, tinv_all)
-    weight = weight_all[...]
-    logits = sharp * dot(smooth_all[...] * weight, same, ((1,), (0,)), highest)
-    smooth_all[...] = logits
+    for slot in range(1, n):
+        place = lse_buf.at[slot]
+        remote(place, place, lsend.at[slot], lrecv.at[slot], "dp", right).wait_recv()
+    parts = [lse_buf[0]] + [pltpu.roll(lse_buf[k], k, 0) for k in range(1, n)]
+    high = functools.reduce(jnp.maximum, parts)
+    totals = high + jnp.log(sum(jnp.exp(part - high) for part in parts))
     for slot in range(n):
         rows = slice(slot * pairs, (slot + 1) * pairs)
-        if slot:
-            place = lse_buf.at[slot]
-            remote(place, place, lsend.at[slot], lrecv.at[slot], "dp", right).wait_recv()
-        share = jnp.exp(smooth_all[rows, :] - lse_buf[slot][0:1])
+        share = jnp.exp(smooth_all[rows, :] - totals[slot : slot + 1])
         slope = OBJECTIVE_FACTOR * sharp * (share - label_all[rows, :])
         tinv_all[rows, :] = weight_all[rows, :] * slope * tinv_all[rows, :]
     grad_doc = jnp.zeros((pairs * DLEN, docs.shape[2]), jnp.float32)
@@ -458,15 +490,15 @@
             pltpu.VMEM((n * pairs, lanes), f32),
             pltpu.VMEM((n * pairs, lanes), f32),
             pltpu.VMEM((n * pairs, lanes), f32),
-            pltpu.VMEM((n, 8, lanes), f32),
+            pltpu.VMEM((n, n, lanes), f32),
             dma((pairs,)),
             dma(()),
             dma((2 * chips, CHUNKS)),
             dma((2 * chips, CHUNKS)),
-            dma((2, n)),
-            dma((n,)),
-            dma((2, n)),
-            dma((n,)),
+            dma((2, n, DOC_CHUNKS)),
+            dma((n, DOC_CHUNKS)),
+            dma((2, n, QUERY_CHUNKS)),
+            dma((n, QUERY_CHUNKS)),
             dma((n,)),
             dma((n,)),
             dma((2, pairs)),

time: 39 us -> 36.6 us (0.938)
  Pallas kernels: 35 us -> 32.5 us
    pallas_call x1, Pallas kernels: 35 us -> 32.5 us  [local(): pl.pallas_call(functools.partial(body, n, sections), out_shape=(jax.Shape...]
where the time goes in v2:
time: 36.6 us; the launch traced here: 36.4 us
  Pallas kernels  32.5 us (89%)
  local copies, waits for them, and re-layouts  3.24 us (9%)
  between operations  0.65 us (2%)
    pallas_call x1, Pallas kernels, local(): pl.pallas_call(functools.partial(body, n, sections), out_shape=(jax.Shape...  32.5 us
    unnamed x4, local copies, waits for them, and re-layouts  3.24 us

profile of v2, /device:TPU:0, one launch (start us, length us, event | category | flops | bytes accessed | tf_op | source)
XLA Modules:
  0.0 36.4 jit_solution(5248502605694147260)
XLA Ops:
  0.6 32.5 %late_interaction.1 = (bf16[1,4,96,2048]{3,2,1,0:T(8,128)(2,1)}, f32[1,4]{1,0:T(1,128)}) custom-call(bf16[1,4,96,2048]{3,2,1,0:T(8,128)(2,1)} %x_hbm.1, f32[1,2048]{1,0:T(1,128)} %bitcast.1, bf16[512,128]{1,0:T(8,128)(2,1)} %w_hbm.1, s32[4,32]{1,0:T(4,128)} %request_ref.1, s32[4,32]{1,0:T(4,128)} %passage_ref.1, s32[4,32]{1,0:T(4,128)} %match_ref.1, f32[2]{0:T(128)} %steep_ref.1), custom_call_target="tpu_custom_call" | custom-call | tf_op jit(solution)/shard_map/late_interaction/pallas_call | solution.py:463
  33.2 0.0 copy-start
  33.2 2.7 %copy.11 = bf16[1,4,96,2048]{3,2,1,0:T(8,128)(2,1)} copy(bf16[1,4,96,2048]{3,2,1,0:T(8,128)(2,1)} %get-tuple-element.4) | data formatting | bytes 3145728
  35.9 0.0 copy-done
  35.9 0.5 %copy.12 = f32[1,4]{1,0:T(1,128)} copy(f32[1,4]{1,0:T(1,128)S(1)} %copy-done) | data formatting | bytes 32
Async XLA Ops:
  33.2 2.7 %copy-start = (f32[1,4]{1,0:T(1,128)S(1)}, f32[1,4]{1,0:T(1,128)}, u32[]{:S(2)}) copy-start(f32[1,4]{1,0:T(1,128)} %get-tuple-element.5) | copy-start | bytes 52

commit v3 on v2

--- a/solution.py
+++ b/solution.py
@@ -15,9 +15,9 @@
 MASKED = -1e30
 
 ROWS = 16
-CHUNKS = 4
-QUERY_CHUNKS = 2
-DOC_CHUNKS = 4
+CHUNKS = 2
+QUERY_CHUNKS = 1
+DOC_CHUNKS = 1
 
 
 def dot(a, b, dims, precision=None):
@@ -36,22 +36,19 @@
     passage_ref,
     match_ref,
     steep_ref,
-    out_hbm,
+    gp_ref,
+    w_all,
     loss_ref,
     xbuf,
     nrm,
     wbuf,
     proj,
-    qinv,
     rinv,
     docs,
     queries,
     e_own,
     e_all,
     gbuf,
-    gqbuf,
-    gnbuf,
-    obuf,
     smooth_own,
     tinv_own,
     smooth_all,
@@ -70,7 +67,6 @@
     qrecv,
     lsend,
     lrecv,
-    osem,
 ):
     pairs, length, width = xbuf.shape
     depth = wbuf.shape[1]
@@ -171,7 +167,6 @@
             v = xbuf[b, pl.ds(r, ROWS), :].astype(jnp.float32)
             q = lax.rsqrt(jnp.sum(v * v, axis=1, keepdims=True) * (1.0 / width) + EPSILON)
             full = pl.multiple_of(b * length + i * ROWS, ROWS)
-            qinv[pl.ds(full, ROWS), :] = jnp.broadcast_to(q, (ROWS, 128))
             z = (v * q * gain).astype(jnp.bfloat16)
             for k in range(sections):
                 nrm[k, pl.ds(full, ROWS), :] = z[:, k * depth : (k + 1) * depth]
@@ -214,6 +209,9 @@
             ).wait_recv()
         add_piece(source)
 
+    w_out = pltpu.make_async_copy(wbuf, w_all, w_sem)
+    w_out.start()
+
     for b in range(pairs):
         p = proj[b * length : (b + 1) * length, :]
         r = lax.rsqrt(jnp.sum(p * p, axis=1, keepdims=True) + EPSILON)
@@ -378,9 +376,6 @@
         ((0,), (0,)),
     )
 
-    all_w = wbuf[...].reshape(sections * depth, wbuf.shape[2])
-    out_copies = []
-
     def head_backward(gradient, first, count):
         for b in range(pairs):
             lo = b * length + first
@@ -388,31 +383,7 @@
             r = rinv[lo : lo + count, :]
             u = proj[lo : lo + count, :] * r
             along = jnp.sum(u * g, axis=1, keepdims=True)
-            gqbuf[b * count : (b + 1) * count, :] = (r * (g - u * along)).astype(jnp.bfloat16)
-        gnbuf[0 : pairs * count, :] = dot(gqbuf[0 : pairs * count, :], all_w, ((1,), (1,)))
-        for b in range(pairs):
-
-            def rows(i, carry, b=b):
-                r = pl.multiple_of(first + i * ROWS, ROWS)
-                v = xbuf[b, pl.ds(r, ROWS), :].astype(jnp.float32)
-                at = pl.multiple_of(b * count + i * ROWS, ROWS)
-                weighted = gnbuf[pl.ds(at, ROWS), :] * gain
-                mean = jnp.sum(v * weighted, axis=1, keepdims=True) * (1.0 / width)
-                full = pl.multiple_of(b * length + first + i * ROWS, ROWS)
-                q = qinv[pl.ds(full, ROWS), :][:, 0:1]
-                obuf[b, pl.ds(r, ROWS), :] = (q * weighted - v * (q * q * q * mean)).astype(
-                    jnp.bfloat16
-                )
-                return carry
-
-            lax.fori_loop(0, count // ROWS, rows, 0, unroll=2)
-            copy = pltpu.make_async_copy(
-                obuf.at[b, pl.ds(first, count)],
-                out_hbm.at[0, b, pl.ds(first, count)],
-                osem.at[0 if first == 0 else 1, b],
-            )
-            copy.start()
-            out_copies.append(copy)
+            gp_ref[lo : lo + count, :] = (r * (g - u * along)).astype(jnp.bfloat16)
 
     head_backward(grad_query, 0, QLEN)
 
@@ -435,8 +406,29 @@
 
     for copy in started:
         copy.wait_send()
-    for copy in out_copies:
-        copy.wait()
+    w_out.wait()
+
+
+def last_body(x_ref, gain_ref, w_ref, gp_ref, loss_in, out_ref, loss_ref, gnbuf):
+    _, _, length, width = x_ref.shape
+    sections, depth, features = w_ref.shape
+    gain = gain_ref[...]
+    all_w = w_ref[...].reshape(sections * depth, features)
+    gnbuf[...] = dot(gp_ref[...], all_w, ((1,), (1,)))
+    loss_ref[...] = loss_in[...]
+
+    def rows(i, carry):
+        r = pl.multiple_of(i * ROWS, ROWS)
+        v = x_ref[0, 0, pl.ds(r, ROWS), :].astype(jnp.float32)
+        weighted = gnbuf[pl.ds(r, ROWS), :] * gain
+        mean = jnp.sum(v * weighted, axis=1, keepdims=True) * (1.0 / width)
+        q = lax.rsqrt(jnp.sum(v * v, axis=1, keepdims=True) * (1.0 / width) + EPSILON)
+        out_ref[0, 0, pl.ds(r, ROWS), :] = (q * weighted - v * (q * q * q * mean)).astype(
+            jnp.bfloat16
+        )
+        return carry
+
+    lax.fori_loop(0, length // ROWS, rows, 0, unroll=True)
 
 
 def local(
@@ -460,29 +452,27 @@
     smem = pl.BlockSpec(memory_space=pltpu.SMEM)
     anywhere = pl.BlockSpec(memory_space=pl.ANY)
     chips = sections // 2
-    return pl.pallas_call(
+    gain = rescale_factor.reshape(1, width)
+    grad_projected, whole_w, loss = pl.pallas_call(
         functools.partial(body, n, sections),
         out_shape=(
-            jax.ShapeDtypeStruct(latent_states.shape, bf16),
+            jax.ShapeDtypeStruct((rows, features), bf16),
+            jax.ShapeDtypeStruct((sections, depth, features), bf16),
             jax.ShapeDtypeStruct((1, pairs), f32),
         ),
         in_specs=[anywhere, vmem, anywhere, smem, smem, smem, smem],
-        out_specs=(anywhere, vmem),
+        out_specs=(vmem, anywhere, vmem),
         scratch_shapes=[
             pltpu.VMEM((pairs, length, width), bf16),
             pltpu.VMEM((sections, rows, depth), bf16),
             pltpu.VMEM((sections, depth, features), bf16),
             pltpu.VMEM((rows, features), f32),
-            pltpu.VMEM((rows, 128), f32),
             pltpu.VMEM((rows, features), f32),
             pltpu.VMEM((n, pairs * DLEN, features), bf16),
             pltpu.VMEM((n, pairs * QLEN, features), bf16),
             pltpu.VMEM((n, pairs * DLEN, lanes), f32),
             pltpu.VMEM((n, pairs * DLEN, lanes), f32),
             pltpu.VMEM((n, pairs * DLEN, lanes), bf16),
-            pltpu.VMEM((pairs * DLEN, features), bf16),
-            pltpu.VMEM((pairs * DLEN, width), f32),
-            pltpu.VMEM((pairs, length, width), bf16),
             pltpu.VMEM((n * pairs, lanes), f32),
             pltpu.VMEM((n * pairs, lanes), f32),
             pltpu.VMEM((n * pairs, lanes), f32),
@@ -501,21 +491,41 @@
             dma((n, QUERY_CHUNKS)),
             dma((n,)),
             dma((n,)),
-            dma((2, pairs)),
-        ],
+                ],
         compiler_params=pltpu.CompilerParams(
             collective_id=0, has_side_effects=True, vmem_limit_bytes=60 * 1024 * 1024
         ),
         name="late_interaction",
     )(
         latent_states,
-        rescale_factor.reshape(1, width),
+        gain,
         embedding_matrix,
         request_span,
         passage_span,
         matching_pair,
         steepness_pair,
     )
+    tokens = pl.BlockSpec((1, 1, length, width), lambda b: (0, b, 0, 0))
+    losses = pl.BlockSpec((1, pairs), lambda b: (0, 0))
+    return pl.pallas_call(
+        last_body,
+        grid=(pairs,),
+        out_shape=(
+            jax.ShapeDtypeStruct(latent_states.shape, bf16),
+            jax.ShapeDtypeStruct((1, pairs), f32),
+        ),
+        in_specs=[
+            tokens,
+            pl.BlockSpec((1, width), lambda b: (0, 0)),
+            pl.BlockSpec((sections, depth, features), lambda b: (0, 0, 0)),
+            pl.BlockSpec((length, features), lambda b: (b, 0)),
+            losses,
+        ],
+        out_specs=(tokens, losses),
+        scratch_shapes=[pltpu.VMEM((length, width), f32)],
+        compiler_params=pltpu.CompilerParams(vmem_limit_bytes=24 * 1024 * 1024),
+        name="head_backward",
+    )(latent_states, gain, whole_w, grad_projected, loss)
 
 
 def solution(mesh):

time: 36.6 us -> 35.5 us (0.970)
  local copies, waits for them, and re-layouts: 3.24 us -> 2.57 us
  Pallas kernels: 32.5 us -> 32 us
    pallas_call x1, Pallas kernels: 32.5 us -> 29.1 us  [local(): pl.pallas_call(functools.partial(body, n, sections), out_shape=(jax.Shape...]
    pallas_call x0 -> x1, Pallas kernels: none -> 2.84 us  [local(): pl.pallas_call(last_body, grid=(pairs,), out_shape=(jax.ShapeDtypeStruct(...]
    unnamed x4 -> x10, local copies, waits for them, and re-layouts: 3.24 us -> 2.57 us
where the time goes in v3:
time: 35.5 us; the launch traced here: 35.2 us
  Pallas kernels  32 us (90%)
  local copies, waits for them, and re-layouts  2.57 us (7%)
  between operations  0.68 us (2%)
    pallas_call x1, Pallas kernels, local(): pl.pallas_call(functools.partial(body, n, sections), out_shape=(jax.Shape...  29.1 us
    pallas_call x1, Pallas kernels, local(): pl.pallas_call(last_body, grid=(pairs,), out_shape=(jax.ShapeDtypeStruct(...  2.84 us
    unnamed x10, local copies, waits for them, and re-layouts  2.57 us

profile of v3, /device:TPU:0, one launch (start us, length us, event | category | flops | bytes accessed | tf_op | source)
XLA Modules:
  0.0 35.2 jit_solution(3410739212851022974)
XLA Ops:
  0.6 0.0 copy-start
  0.6 0.0 copy-start.3
  0.7 29.1 %late_interaction.1 = (bf16[384,128]{1,0:T(8,128)(2,1)}, bf16[4,512,128]{2,1,0:T(8,128)(2,1)}, f32[1,4]{1,0:T(1,128)}) custom-call(bf16[1,4,96,2048]{3,2,1,0:T(8,128)(2,1)} %x_ref.1, f32[1,2048]{1,0:T(1,128)} %bitcast.1, bf16[512,128]{1,0:T(8,128)(2,1)} %w_hbm.1, s32[4,32]{1,0:T(4,128)} %request_ref.1, s32[4,32]{1,0:T(4,128)} %passage_ref.1, ...), custom_call_target="tpu_custom_call" | custom-call | tf_op jit(solution)/shard_map/late_interaction/pallas_call | solution.py:456
  29.8 0.0 copy-done
  29.8 0.0 copy-done.3
  29.8 0.0 copy-start.1
  29.8 1.0 %copy-done.1 = bf16[4,512,128]{2,1,0:T(8,128)(2,1)S(1)} copy-done((bf16[4,512,128]{2,1,0:T(8,128)(2,1)S(1)}, bf16[4,512,128]{2,1,0:T(8,128)(2,1)}, u32[]{:S(2)}) %copy-start.1) | copy-done | bytes 524312
  30.9 0.0 copy-start.2
  30.9 0.9 %copy-done.2 = bf16[384,128]{1,0:T(8,128)(2,1)S(1)} copy-done((bf16[384,128]{1,0:T(8,128)(2,1)S(1)}, bf16[384,128]{1,0:T(8,128)(2,1)}, u32[]{:S(2)}) %copy-start.2) | copy-done | bytes 98328
  31.8 0.0 copy-start.4
  31.8 0.6 %copy-done.4 = f32[1,4]{1,0:T(1,128)S(1)} copy-done((f32[1,4]{1,0:T(1,128)S(1)}, f32[1,4]{1,0:T(1,128)}, u32[]{:S(2)}) %copy-start.4) | copy-done | bytes 40
  32.4 2.8 %head_backward.1 = (bf16[1,4,96,2048]{3,2,1,0:T(8,128)(2,1)}, f32[1,4]{1,0:T(1,128)}) custom-call(bf16[1,4,96,2048]{3,2,1,0:T(8,128)(2,1)S(1)} %copy-done, f32[1,2048]{1,0:T(1,128)S(1)} %bitcast.2, bf16[4,512,128]{2,1,0:T(8,128)(2,1)S(1)} %copy-done.1, bf16[384,128]{1,0:T(8,128)(2,1)S(1)} %copy-done.2, f32[1,4]{1,0:T(1,128)S(1)} %copy-done.4), custom_call_target="tpu_custom_call" | custom-call | tf_op jit(solution)/shard_map/head_backward/pallas_call | solution.py:510
Async XLA Ops:
  0.6 29.2 %copy-start = (bf16[1,4,96,2048]{3,2,1,0:T(8,128)(2,1)S(1)}, bf16[1,4,96,2048]{3,2,1,0:T(8,128)(2,1)}, u32[]{:S(2)}) copy-start(bf16[1,4,96,2048]{3,2,1,0:T(8,128)(2,1)} %x_ref.1) | copy-start | bytes 4718596
  0.6 29.2 %copy-start.3 = (f32[2048]{0:T(1024)S(1)}, f32[2048]{0:T(1024)}, u32[]{:S(2)}) copy-start(f32[2048]{0:T(1024)} %param.8) | copy-start | bytes 24580
  29.8 1.0 %copy-start.1 = (bf16[4,512,128]{2,1,0:T(8,128)(2,1)S(1)}, bf16[4,512,128]{2,1,0:T(8,128)(2,1)}, u32[]{:S(2)}) copy-start(bf16[4,512,128]{2,1,0:T(8,128)(2,1)} %get-tuple-element.5.w_ref) | copy-start | bytes 1572868
  30.9 0.9 %copy-start.2 = (bf16[384,128]{1,0:T(8,128)(2,1)S(1)}, bf16[384,128]{1,0:T(8,128)(2,1)}, u32[]{:S(2)}) copy-start(bf16[384,128]{1,0:T(8,128)(2,1)} %get-tuple-element.6.gp_ref) | copy-start | bytes 294916
  31.8 0.6 %copy-start.4 = (f32[1,4]{1,0:T(1,128)S(1)}, f32[1,4]{1,0:T(1,128)}, u32[]{:S(2)}) copy-start(f32[1,4]{1,0:T(1,128)} %get-tuple-element.7.loss_in) | copy-start | bytes 52

commit v4 on v3

--- a/solution.py
+++ b/solution.py
@@ -409,12 +409,27 @@
     w_out.wait()
 
 
-def last_body(x_ref, gain_ref, w_ref, gp_ref, loss_in, out_ref, loss_ref, gnbuf):
+def last_body(
+    x_ref, gain_ref, w_hbm, gp_hbm, loss_hbm, out_ref, loss_ref, gnbuf, w_ref, gp_ref, loss_in, sem
+):
+    @pl.when(pl.program_id(0) == 0)
+    def _():
+        copies = [
+            pltpu.make_async_copy(w_hbm, w_ref, sem.at[0]),
+            pltpu.make_async_copy(gp_hbm, gp_ref, sem.at[1]),
+            pltpu.make_async_copy(loss_hbm, loss_in, sem.at[2]),
+        ]
+        for copy in copies:
+            copy.start()
+        for copy in copies:
+            copy.wait()
+
     _, _, length, width = x_ref.shape
     sections, depth, features = w_ref.shape
     gain = gain_ref[...]
     all_w = w_ref[...].reshape(sections * depth, features)
-    gnbuf[...] = dot(gp_ref[...], all_w, ((1,), (1,)))
+    first = pl.multiple_of(pl.program_id(0) * length, ROWS)
+    gnbuf[...] = dot(gp_ref[pl.ds(first, length), :], all_w, ((1,), (1,)))
     loss_ref[...] = loss_in[...]
 
     def rows(i, carry):
@@ -517,13 +532,19 @@
         in_specs=[
             tokens,
             pl.BlockSpec((1, width), lambda b: (0, 0)),
-            pl.BlockSpec((sections, depth, features), lambda b: (0, 0, 0)),
-            pl.BlockSpec((length, features), lambda b: (b, 0)),
-            losses,
+            pl.BlockSpec(memory_space=pltpu.HBM),
+            pl.BlockSpec(memory_space=pltpu.HBM),
+            pl.BlockSpec(memory_space=pltpu.HBM),
         ],
         out_specs=(tokens, losses),
-        scratch_shapes=[pltpu.VMEM((length, width), f32)],
-        compiler_params=pltpu.CompilerParams(vmem_limit_bytes=24 * 1024 * 1024),
+        scratch_shapes=[
+            pltpu.VMEM((length, width), f32),
+            pltpu.VMEM((sections, depth, features), bf16),
+            pltpu.VMEM((rows, features), bf16),
+            pltpu.VMEM((1, pairs), f32),
+            dma((3,)),
+        ],
+        compiler_params=pltpu.CompilerParams(vmem_limit_bytes=67043328),
         name="head_backward",
     )(latent_states, gain, whole_w, grad_projected, loss)
 

time: 35.5 us -> 35.6 us (level)
  Pallas kernels: 32 us -> 34.7 us
  local copies, waits for them, and re-layouts: 2.57 us -> 0 us
    pallas_call x1, Pallas kernels: 2.84 us -> 5.52 us  [local(): pl.pallas_call(last_body, grid=(pairs,), out_shape=(jax.ShapeDtypeStruct(...]
    unnamed x10 -> x0, local copies, waits for them, and re-layouts: 2.57 us -> none
where the time goes in v4:
time: 35.6 us; the launch traced here: 35.3 us
  Pallas kernels  34.7 us (97%)
  between operations  0.64 us (2%)
    pallas_call x1, Pallas kernels, local(): pl.pallas_call(functools.partial(body, n, sections), out_shape=(jax.Shape...  29.1 us
    pallas_call x1, Pallas kernels, local(): pl.pallas_call(last_body, grid=(pairs,), out_shape=(jax.ShapeDtypeStruct(...  5.52 us

profile of v4, /device:TPU:0, one launch (start us, length us, event | category | flops | bytes accessed | tf_op | source)
XLA Modules:
  0.0 35.3 jit_solution(14182989952962791728)
XLA Ops:
  0.6 29.1 %late_interaction.1 = (bf16[384,128]{1,0:T(8,128)(2,1)}, bf16[4,512,128]{2,1,0:T(8,128)(2,1)}, f32[1,4]{1,0:T(1,128)}) custom-call(bf16[1,4,96,2048]{3,2,1,0:T(8,128)(2,1)} %x_ref.1, f32[1,2048]{1,0:T(1,128)} %bitcast.1, bf16[512,128]{1,0:T(8,128)(2,1)} %w_hbm.1, s32[4,32]{1,0:T(4,128)} %request_ref.1, s32[4,32]{1,0:T(4,128)} %passage_ref.1, ...), custom_call_target="tpu_custom_call" | custom-call | tf_op jit(solution)/shard_map/late_interaction/pallas_call | solution.py:471
  29.8 5.5 %head_backward.1 = (bf16[1,4,96,2048]{3,2,1,0:T(8,128)(2,1)}, f32[1,4]{1,0:T(1,128)}) custom-call(bf16[1,4,96,2048]{3,2,1,0:T(8,128)(2,1)} %x_ref.1, f32[1,2048]{1,0:T(1,128)} %bitcast.2, bf16[4,512,128]{2,1,0:T(8,128)(2,1)} %get-tuple-element.5.w_hbm, bf16[384,128]{1,0:T(8,128)(2,1)} %get-tuple-element.6.gp_hbm, f32[1,4]{1,0:T(1,128)} %get-tuple-element.7.loss_hbm), custom_call_target="tpu_custom_call" | custom-call | tf_op jit(solution)/shard_map/head_backward/pallas_call | solution.py:525
